TPU v7x, 128 devices: a whole 4x4x4 slice. The times are simulated.
128 devices in a mesh: req: 16 (over z, y), mlp: 8 (over x, core).
Axes of the slice: x: 4, y: 4, z: 4, core: 2. Of those that a mesh axis runs over, the one named last changes fastest.
Arguments:
- hidden: bfloat16 [8192, 3584], P('req', 'mlp'), may hold values from -6 to 6
- query_heads: bfloat16 [8192, 3584], P('req', 'mlp'), may hold values from -4 to 4
- key_heads: bfloat16 [8192, 3584], P('req', 'mlp'), may hold values from -4 to 4
- value_heads: bfloat16 [8192, 3584], P('req', 'mlp'), may hold values from -6 to 6
- segment_ids: int32 [8192], P('req'), may hold values from 0 to 63, never falling along the last dimension, each value on 1 to 1024 neighbouring positions
- page_table: int32 [16, 32], P('req'), may hold values from 0 to 31, each once within a row
- mamba_conv_input: bfloat16 [8192, 7168], P('req', 'mlp'), may hold values from -6 to 6
- mamba_output_gate: bfloat16 [8192, 7168], P('req', 'mlp'), may hold values from -6 to 6
- state_input_projection: bfloat16 [8192, 128], P('req'), may hold values from -6 to 6
- state_output_projection: bfloat16 [8192, 128], P('req'), may hold values from -6 to 6
- discrete_step_size: float32 [8192, 112], P('req', 'mlp'), may hold values from 0.24 to 100, as said below
- head_decay_rate: float32 [112], P('mlp'), may hold values from 0.00024414062 to 0.05, as said below
- skip_gain: float32 [112], P('mlp'), may hold values from 0.5 to 2
- mamba_gated_norm_gain: float32 [7168], P('mlp'), may hold values from 0.1 to 1.9
- attn_proj: bfloat16 [3584, 3584], P('mlp'), may hold values from -0.09375 to 0.09375
- mamba_output_projection: bfloat16 [7168, 3584], P('mlp'), may hold values from -0.0625 to 0.0625
- mlp_norm_gain: float32 [3584], replicated, may hold values from 0.1 to 1.9
- gate_proj: bfloat16 [3584, 7168], P('req', 'mlp'), may hold values from -0.09375 to 0.09375
- up_proj: bfloat16 [3584, 7168], P('req', 'mlp'), may hold values from -0.09375 to 0.09375
- down_proj: bfloat16 [7168, 3584], P('mlp', 'req'), may hold values from -0.0625 to 0.0625
- next_norm_gain: float32 [3584], P('mlp'), may hold values from 0.1 to 1.9
Outputs:
- new_hidden: bfloat16 [8192, 3584], P('req', 'mlp')
- next_normed: bfloat16 [8192, 3584], P('req', 'mlp')
- kv_cache: bfloat16 [2, 16, 512, 3584], P(None, 'mlp', 'req')
Inputs may be any that keep to these rules, and one draw needn't show every extreme that they name: `segment_ids`: prompt ids never fall along the stream; a prompt has 1 to 1024 tokens and one has exactly 1024. `page_table`: each request group's row names every page of its pool once. `discrete_step_size`: Positive. `head_decay_rate`: Positive.
All inputs are finite; a program needn't handle non-finite values.
Results may differ from a plain program's by a relative error of at most 0.006.
Values may be sent and summed in bfloat16 or wider, within the bound.
No kernel may reach another device: no remote copies, remote signals or barrier semaphores. Data moves between devices by JAX's collectives and lax.ppermute only.
A program may use at most 128 MiB of HBM per device.

v0:
```python
import math
import jax
import jax.numpy as jnp
from jax import lax
from jax.sharding import PartitionSpec as P

HD = 224
MAMBA_HEAD_COUNT = 112
MAMBA_HEAD_SIZE = 64
STATE_SIZE = 64
STATE_GROUPS = 2
REACH = 2
PAGE = 16
EPSILON = 1e-05
exact_mode = lax.Precision.HIGHEST


def from_behind(value, axis, steps):
    count = lax.axis_size(axis)
    leading, last = (max(0, -steps), min(count, count - steps))
    return lax.ppermute(value, axis, [(source, source + steps) for source in range(leading, last)])


def entering(x, axis, combine, identity):
    devices, mine = (lax.axis_size(axis), lax.axis_index(axis))
    everything = jax.tree.map(lambda part: lax.all_gather(part, axis), x)
    start = jax.tree.map(
        lambda part, zero: jnp.broadcast_to(jnp.asarray(zero, part.dtype), part.shape), x, identity
    )

    def step(k, before):
        reached = k < mine
        new = combine(before, jax.tree.map(lambda part: part[k], everything))
        return jax.tree.map(lambda a, b: jnp.where(reached, a, b), new, before)

    return lax.fori_loop(0, devices, step, start)


def attend_rows(
    query_rows, segment_rows, pos_rows, all_keys, all_values, key_segs, key_pos, head_count
):
    row_total = query_rows.shape[0]
    key_total = all_keys.shape[0]
    query_split = query_rows.reshape(row_total, head_count, HD)
    key_split = all_keys.reshape(key_total, head_count, HD)
    value_split = all_values.reshape(key_total, head_count, HD)
    scores = jnp.einsum(
        "qhd,khd->hqk", query_split, key_split, preferred_element_type=jnp.float32
    ) * (1.0 / math.sqrt(HD))
    allowed = (segment_rows[:, None] == key_segs[None, :]) & (key_pos[None, :] <= pos_rows[:, None])
    scores = jnp.where(allowed[None, :, :], scores, -jnp.inf)
    top_score = jnp.max(scores, axis=2, keepdims=True)
    raised = jnp.exp(scores - top_score)
    weights = (raised / jnp.sum(raised, axis=2, keepdims=True)).astype(jnp.bfloat16)
    summed = jnp.einsum("hqk,khd->qhd", weights, value_split, preferred_element_type=jnp.float32)
    return summed.astype(jnp.bfloat16).reshape(row_total, head_count * HD)


def block_contributions(
    input_token_rows,
    input_proj_rows,
    output_proj_rows,
    step_size_rows,
    head_decay_rate,
    segment_rows,
    segment_prior_state,
    group_index,
    head_width,
):
    row_count = input_token_rows.shape[0]
    head_count = step_size_rows.shape[1]
    input_float = input_token_rows.astype(jnp.float32).reshape(row_count, head_count, head_width)
    b_float = input_proj_rows.astype(jnp.float32)
    c_float = output_proj_rows.astype(jnp.float32)
    running = jnp.cumsum(-step_size_rows * head_decay_rate[None, :], axis=0)
    positions = jnp.arange(row_count, dtype=jnp.int32)
    live = (segment_rows[:, None] == segment_rows[None, :]) & (
        positions[:, None] >= positions[None, :]
    )
    spread = running.T[:, :, None] - running.T[:, None, :]
    mixing = jnp.exp(jnp.where(live[None, :, :], spread, -1e30))
    inner = jnp.einsum("tgn,ugn->gtu", c_float, b_float, precision=exact_mode)
    driven = input_float * step_size_rows[:, :, None]
    local_output = jnp.einsum(
        "htu,uhp->thp", mixing * inner[group_index], driven, precision=exact_mode
    )
    b_per_head = b_float[:, group_index, :]
    output_proj_per_head = c_float[:, group_index, :]
    tail_rows = segment_rows == segment_rows[row_count - 1]
    tail_gain = jnp.where(
        tail_rows[:, None], jnp.exp(running[row_count - 1][None, :] - running), 0.0
    )
    state_local_part = jnp.einsum(
        "uh,uhp,uhn->hpn", tail_gain, driven, b_per_head, precision=exact_mode
    )
    decay_cumulative = jnp.where(
        segment_rows[row_count - 1] == segment_prior_state, jnp.exp(running[row_count - 1]), 0.0
    )
    entry_weighting = jnp.where(
        (segment_rows == segment_prior_state)[:, None], jnp.exp(running), 0.0
    )
    return (
        local_output,
        decay_cumulative,
        state_local_part,
        entry_weighting,
        input_float,
        output_proj_per_head,
    )


def finish(local_output, entry_weighting, input_float, output_proj_per_head, carry_in, skip_gain):
    carried = jnp.einsum("hpn,thn->thp", carry_in, output_proj_per_head, precision=exact_mode)
    result = (
        local_output
        + entry_weighting[:, :, None] * carried
        + skip_gain[None, :, None] * input_float
    )
    return result.reshape(result.shape[0], result.shape[1] * result.shape[2])


def merge_states(earlier, later):
    decay_early, state_early = earlier
    decay_late, state_late = later
    return (decay_early * decay_late, decay_late[:, None, None] * state_early + state_late)


def body(
    hidden,
    query_heads,
    key_heads,
    value_heads,
    segment_ids,
    page_table,
    mamba_conv_input,
    mamba_output_gate,
    state_input_projection,
    state_output_projection,
    discrete_step_size,
    head_decay_rate,
    skip_gain,
    mamba_gated_norm_gain,
    attn_proj,
    mamba_output_projection,
    mlp_norm_gain,
    gate_proj,
    up_proj,
    down_proj,
    next_norm_gain,
):
    row_count = query_heads.shape[0]
    head_count = query_heads.shape[1] // HD
    lane_count = hidden.shape[1]
    owner_index = lax.axis_index("req")
    column = lax.axis_index("mlp")
    first_row = owner_index * row_count
    lead_rows = REACH * row_count
    shifted_ids = segment_ids + 1
    key_parts = []
    value_parts = []
    segment_parts = []
    for distance in range(REACH, 0, -1):
        moved_ids = from_behind(shifted_ids, "req", distance)
        segment_parts.append(moved_ids - 1)
        moved_keys, moved_values = from_behind((key_heads, value_heads), "req", distance)
        key_parts.append(moved_keys)
        value_parts.append(moved_values)
    key_segs = jnp.concatenate(segment_parts + [segment_ids], axis=0)
    key_pos = first_row - lead_rows + jnp.arange(lead_rows + row_count, dtype=jnp.int32)
    segment_prior_state = segment_parts[-1][row_count - 1]
    all_keys = jnp.concatenate(key_parts + [key_heads], axis=0)
    all_values = jnp.concatenate(value_parts + [value_heads], axis=0)
    block_rows = min(row_count, 512)

    def one_block(block_index):
        first_local = block_index * block_rows
        pos_rows = first_row + first_local + jnp.arange(block_rows, dtype=jnp.int32)
        return attend_rows(
            query_heads, segment_ids, pos_rows, all_keys, all_values, key_segs, key_pos, head_count
        )

    attended = lax.map(one_block, jnp.arange(row_count // block_rows, dtype=jnp.int32)).reshape(
        row_count, head_count * HD
    )
    page_count = page_table.shape[1]
    key_pages = (
        key_heads.reshape(page_count, PAGE, head_count, HD)
        .transpose(2, 0, 1, 3)
        .reshape(head_count, page_count, PAGE * HD)
    )
    value_pages = (
        value_heads.reshape(page_count, PAGE, head_count, HD)
        .transpose(2, 0, 1, 3)
        .reshape(head_count, page_count, PAGE * HD)
    )
    stacked = jnp.stack([key_pages, value_pages])
    kv_cache = jnp.zeros_like(stacked).at[:, :, page_table[0]].set(stacked)
    mamba_heads = discrete_step_size.shape[1]
    group_values = MAMBA_HEAD_COUNT // STATE_GROUPS
    b_groups = state_input_projection.reshape(row_count, STATE_GROUPS, STATE_SIZE)
    c_groups = state_output_projection.reshape(row_count, STATE_GROUPS, STATE_SIZE)
    group_index = jnp.arange(mamba_heads, dtype=jnp.int32) % STATE_GROUPS
    (
        local_output,
        decay_cumulative,
        state_local_part,
        entry_weighting,
        input_float,
        output_proj_per_head,
    ) = block_contributions(
        mamba_conv_input,
        b_groups,
        c_groups,
        discrete_step_size,
        head_decay_rate,
        segment_ids,
        segment_prior_state,
        group_index,
        MAMBA_HEAD_SIZE,
    )
    unused_decay, carry_in = entering(
        (decay_cumulative, state_local_part),
        "req",
        merge_states,
        (jnp.ones_like(decay_cumulative), jnp.zeros_like(state_local_part)),
    )
    mamba_output = finish(
        local_output, entry_weighting, input_float, output_proj_per_head, carry_in, skip_gain
    )
    gated_output = mamba_output * jax.nn.silu(mamba_output_gate.astype(jnp.float32))
    grouped_values = gated_output.reshape(
        row_count, mamba_heads // STATE_GROUPS, STATE_GROUPS, MAMBA_HEAD_SIZE
    )
    group_squares = jnp.sum(grouped_values * grouped_values, axis=(1, 3))
    running_totals = lax.psum(group_squares, "mlp")
    inverse_group = lax.rsqrt(running_totals / (group_values * MAMBA_HEAD_SIZE) + EPSILON)
    mnormed = (
        (grouped_values * inverse_group[:, None, :, None]).reshape(
            row_count, mamba_heads * MAMBA_HEAD_SIZE
        )
        * mamba_gated_norm_gain[None, :]
    ).astype(jnp.bfloat16)
    projected = jnp.dot(attended, attn_proj, preferred_element_type=jnp.float32) + jnp.dot(
        mnormed, mamba_output_projection, preferred_element_type=jnp.float32
    )
    width_total = projected.shape[1]
    offset = column * lane_count
    own_part = lax.dynamic_slice_in_dim(projected, offset, lane_count, 1) + hidden.astype(
        jnp.float32
    )
    mixed_rows = lax.psum(lax.dynamic_update_slice_in_dim(projected, own_part, offset, 1), "mlp")
    mixed_share = lax.dynamic_slice_in_dim(mixed_rows, offset, lane_count, 1)
    inverse_root_mean = lax.rsqrt(jnp.mean(mixed_rows * mixed_rows, axis=1) + EPSILON)
    normed = (mixed_rows * inverse_root_mean[:, None] * mlp_norm_gain[None, :]).astype(jnp.bfloat16)
    gate_act = jnp.dot(
        normed,
        lax.all_gather(gate_proj, "req", axis=0, tiled=True),
        preferred_element_type=jnp.float32,
    )
    up_act = jnp.dot(
        normed,
        lax.all_gather(up_proj, "req", axis=0, tiled=True),
        preferred_element_type=jnp.float32,
    )
    latent_activation = (jax.nn.silu(gate_act) * up_act).astype(jnp.bfloat16)
    partial_value = jnp.dot(
        latent_activation,
        lax.all_gather(down_proj, "req", axis=1, tiled=True),
        preferred_element_type=jnp.float32,
    )
    mlp_share = lax.psum_scatter(partial_value, "mlp", scatter_dimension=1, tiled=True)
    new_hidden = (mixed_share + mlp_share).astype(jnp.bfloat16)
    widened = new_hidden.astype(jnp.float32)
    total_sq = lax.psum(jnp.sum(widened * widened, axis=1), "mlp")
    next_normed = (
        widened * lax.rsqrt(total_sq / width_total + EPSILON)[:, None] * next_norm_gain[None, :]
    ).astype(jnp.bfloat16)
    return (new_hidden, next_normed, kv_cache)


def solution(mesh):
    return jax.shard_map(
        body,
        mesh=mesh,
        in_specs=(
            P("req", "mlp"),
            P("req", "mlp"),
            P("req", "mlp"),
            P("req", "mlp"),
            P("req"),
            P("req", None),
            P("req", "mlp"),
            P("req", "mlp"),
            P("req", None),
            P("req", None),
            P("req", "mlp"),
            P("mlp"),
            P("mlp"),
            P("mlp"),
            P("mlp", None),
            P("mlp", None),
            P(),
            P("req", "mlp"),
            P("req", "mlp"),
            P("mlp", "req"),
            P("mlp"),
        ),
        out_specs=(P("req", "mlp"), P("req", "mlp"), P(None, "mlp", "req", None)),
        check_vma=False,
    )
```

profile of v0, /device:TPU:0, one launch (start us, length us, event | category | flops | bytes accessed | tf_op | source)
XLA Modules:
  0.0 616.1 jit_solution(2052999723825984348)
XLA Ops:
  8.7 3.6 collective-permute-start.3
  16.9 2.5 copy.75
  19.4 1.5 gather_fusion.2
  25.6 3.5 fusion.22
  29.2 5.4 collective-permute-start.2
  34.6 4.1 collective-permute-start.4
  38.7 4.3 collective-permute-start.5
  43.0 4.0 collective-permute-start
  47.0 3.6 collective-permute-start.1
  52.6 1.8 fusion.59
  54.4 1.7 gather_fusion.1
  56.1 8.8 %gather_fusion = f32[14,512,512]{2,1,0:T(8,128)} fusion(f32[2,512,512]{2,1,0:T(8,128)} %fusion.59, s32[1024]{0:T(1024)} %copy-done.13), kind=kCustom, calls=%fused_computation | custom fusion | bytes 29360184 | tf_op jit(solution)/shard_map/gather | solution.py:85
  64.9 2.0 copy.83
  67.7 1.9 compare_and_fusion
  69.6 39.1 %all-gather.1 = f32[16,1,14]{2,1,0:T(1,128)S(1)} all-gather(f32[1,1,14]{2,1,0:T(1,128)S(1)} %bitcast.114), channel_id=1, replica_groups=mesh['req'=16,'mlp'=8] {'req'}, dimensions={0}, use_global_device_ids=true | all-gather | bytes 952 | tf_op jit(solution)/shard_map/all_gather | solution.py:26
  108.7 2.5 pad_maximum_fusion.1
  111.3 2.3 pad_maximum_fusion
  113.6 4.1 fusion.58
  117.7 6.2 %fusion.30 = bf16[2,224,512]{2,1,0:T(8,128)(2,1)} fusion(bf16[1536,2,224]{0,2,1:T(8,128)(2,1)} %bitcast.105, f32[2,512]{1,0:T(2,128)S(1)} %fusion.58, pred[512,1536]{0,1:T(8,128)(4,1)} %compare_and_fusion, bf16[1536,2,224]{0,2,1:T(8,128)(2,1)} %bitcast.104, bf16[512,2,224]{0,2,1:T(8,128)(2,1)} %bitcast.116), kind=kOutput, calls=%fused_computation.49 | convolution fusion | flops 1417382400 | bytes 4460544 | tf_op jit(solution)/shard_map/while/body/eval_jaxpr/hqk,khd->qhd/dot_general | solution.py:55
  123.9 43.8 %while.18 = (s32[]{:T(128)}, f32[14,64,64]{2,1,0:T(8,128)}, s32[]{:T(128)}, f32[16,14]{1,0:T(8,128)S(1)}, f32[16,14,64,64]{3,2,1,0:T(8,128)}, /*index=5*/s32[]{:T(128)}, s32[]{:T(128)}) while((s32[]{:T(128)}, f32[14,64,64]{2,1,0:T(8,128)}, s32[]{:T(128)}, f32[16,14]{1,0:T(8,128)S(1)}, f32[16,14,64,64]{3,2,1,0:T(8,128)}, ...), condition=%wide.region_5.6_spmd.clone, body=%wide.region_4.5_spmd.clone.sunk | while | flops 229380 | bytes 688401 | solution.py:36
  135.0 1.9 fusion.75
  136.9 2.0 fusion.75
  138.9 2.0 fusion.75
  141.0 2.0 fusion.75
  143.0 2.0 fusion.75
  145.1 2.0 fusion.75
  147.1 2.0 fusion.75
  149.2 2.0 fusion.75
  151.2 2.0 fusion.75
  153.3 2.0 fusion.75
  155.3 2.0 fusion.75
  157.4 2.0 fusion.75
  159.4 2.0 fusion.75
  161.5 2.0 fusion.75
  163.5 2.0 fusion.75
  165.6 2.0 fusion.75
  167.7 2.3 fusion.37
  170.0 20.4 %fusion.21 = f32[512,14,64]{0,2,1:T(8,128)} fusion(f32[14,512,64]{1,2,0:T(8,128)S(1)} %fusion.37, f32[512,14,64]{0,2,1:T(8,128)S(1)} %bitcast.98, f32[14,512,512]{2,1,0:T(8,128)} %gather_fusion, f32[14,512]{1,0:T(8,128)S(1)} %bitcast.111, pred[512,512]{1,0:T(8,128)(4,1)S(1)} %copy-done.9, f32[14]{0:T(128)S(1)} %copy-done.18, f32[512,14]{0,1:T(8,128)S(1)} %copy-done.12, ...), kind=kOutput, calls=%fused_computation.38 | convolution fusion | flops 2831876096 | bytes 20533304 | tf_op jit(solution)/shard_map/htu,uhp->thp/dot_general | solution.py:84
  190.5 2.8 copy.80
  193.2 3.4 fusion.56
  196.7 2.8 copy.81
  199.5 1.6 reduce_sum.38
  201.1 12.4 %psum.21 = f32[512,2]{0,1:T(2,128)S(1)} all-reduce(f32[512,2]{0,1:T(2,128)S(1)} %reduce_sum.38), channel_id=1, replica_groups=mesh['req'=16,'mlp'=8] {'mlp'}, use_global_device_ids=true, to_apply=%region_7.8 | all-reduce | flops 1024 | bytes 8192 | tf_op jit(solution)/shard_map/psum | solution.py:235
  213.5 1.5 mul.166
  215.0 2.7 copy.82
  217.8 8.2 %fusion.35 = f32[512,3584]{1,0:T(8,128)S(1)} fusion(bf16[896,3584]{1,0:T(8,128)(2,1)} %param.38, f32[512,896]{1,0:T(8,128)} %copy.82, f32[896]{0:T(1024)S(1)} %copy-done.17, f32[512,896]{1,0:T(8,128)} %copy.80, bf16[512,896]{1,0:T(8,128)(2,1)} %param.30), kind=kOutput, calls=%fused_computation.57 | convolution fusion | flops 3292463104 | bytes 18353664 | tf_op jit(solution)/shard_map/dot_general | solution.py:243
  226.0 2.2 convolution_add_fusion
  228.2 3.0 copy-done.2
  231.5 5.8 dynamic_update_slice.6
  239.3 88.7 %all-reduce.2.cloned.1.call-done = f32[512,3584]{1,0:T(8,128)} async-done(((f32[512,3584]{1,0:T(8,128)}), f32[512,3584]{1,0:T(8,128)}) %all-reduce.2.cloned.1.call-update) | async-done | bytes 7340048 | tf_op jit(solution)/shard_map/psum | solution.py:251
  328.1 3.6 multiply_reduce_fusion
  331.7 60.3 %all-gather.7.cloned.1.call-done = bf16[3584,896]{1,0:T(8,128)(2,1)} async-done(((bf16[224,896]{1,0:T(8,128)(2,1)}), bf16[3584,896]{1,0:T(8,128)(2,1)}) %all-gather.7.cloned.1.call-update) | async-done | bytes 6422544 | tf_op jit(solution)/shard_map/all_gather | solution.py:257
  392.0 8.4 %fusion.57 = f32[512,896]{1,0:T(8,128)S(1)} fusion(bf16[3584,896]{1,0:T(8,128)(2,1)} %all-gather.7.cloned.1.call-done, f32[512,3584]{1,0:T(8,128)} %all-reduce.2.cloned.1.call-done, f32[3584]{0:T(1024)S(1)} %copy-done.16, f32[512]{0:T(512)S(1)} %add_rsqrt_fusion.2), kind=kOutput, calls=%fused_computation.98 | convolution fusion | flops 3293839360 | bytes 15613952 | tf_op jit(solution)/shard_map/dot_general | solution.py:255
  400.5 55.1 %all-gather.11.cloned.1.call-done = bf16[896,3584]{0,1:T(8,128)(2,1)} async-done(((bf16[896,224]{0,1:T(8,128)(2,1)}), bf16[896,3584]{0,1:T(8,128)(2,1)}) %all-gather.11.cloned.1.call-update) | async-done | bytes 6422544 | tf_op jit(solution)/shard_map/all_gather | solution.py:268
  455.6 63.6 %all-gather.9.cloned.1.call-done = bf16[3584,896]{1,0:T(8,128)(2,1)} async-done(((bf16[224,896]{1,0:T(8,128)(2,1)}), bf16[3584,896]{1,0:T(8,128)(2,1)}) %all-gather.9.cloned.1.call-update) | async-done | bytes 6422544 | tf_op jit(solution)/shard_map/all_gather | solution.py:262
  519.2 17.7 %convolution_bitcast_fusion = f32[3584,512]{1,0:T(8,128)} fusion(bf16[896,3584]{0,1:T(8,128)(2,1)} %all-gather.11.cloned.1.call-done, f32[512,896]{1,0:T(8,128)S(1)} %fusion.57, bf16[3584,896]{1,0:T(8,128)(2,1)} %all-gather.9.cloned.1.call-done, f32[512,3584]{1,0:T(8,128)} %all-reduce.2.cloned.1.call-done, f32[3584]{0:T(1024)S(1)} %copy-done.16, ...), kind=kOutput, calls=%fused_computation.19 | convolution fusion | flops 6584926208 | bytes 29376512
  542.5 2.6 scatter_fusion
  546.0 38.0 %reduce-scatter.4.cloned.1.call-done = f32[448,512]{1,0:T(8,128)} async-done(((f32[3584,512]{1,0:T(8,128)}), f32[448,512]{1,0:T(8,128)}) %reduce-scatter.4.cloned.1.call-update) | async-done | bytes 917520
  584.1 2.7 copy.96
  586.7 2.8 fusion.31
  589.6 13.2 %psum.23 = f32[512]{0:T(512)S(1)} all-reduce(f32[512]{0:T(512)S(1)} %get-tuple-element.167), channel_id=1, replica_groups=mesh['req'=16,'mlp'=8] {'mlp'}, use_global_device_ids=true, to_apply=%region_12.13 | all-reduce | flops 512 | bytes 4096 | tf_op jit(solution)/shard_map/psum | solution.py:274
  602.8 2.0 copy.90
  604.8 2.0 fusion.33
  606.8 2.0 copy.91
  (119 shorter events, 21.0 us)
Async XLA Ops:
  7.2 218.8 %copy-start = (bf16[448,3584]{1,0:T(8,128)(2,1)S(1)}, bf16[448,3584]{1,0:T(8,128)(2,1)}, u32[]{:S(2)}) copy-start(bf16[448,3584]{1,0:T(8,128)(2,1)} %param.37) | copy-start | bytes 9633796
  7.2 116.7 %all-gather.13.cloned.1.call-start = ((), (), s32[]{:S(2)}) async-start(), calls=%async_computation.5 | async-start | bytes 7798784 | tf_op jit(solution)/shard_map/all_gather | solution.py:26
  8.7 12.3 %collective-permute-start.3 = (s32[512]{0:T(512)}, s32[512]{0:T(512)S(1)}, u32[]{:S(2)}, u32[]{:S(2)}) collective-permute-start(s32[512]{0:T(512)} %broadcast_add_fusion.3), channel_id=1, source_target_pairs={{0,8},{8,16},{16,24},{24,32},{32,40},{40,48},{48,56},{56,64},{64,7... | collective-permute-start | bytes 6152 | tf_op jit(solution)/shard_map/ppermute | solution.py:21
  14.5 6.4 %copy-start.13 = (s32[1024]{0:T(1024)}, s32[1024]{0:T(1024)S(1)}, u32[]{:S(2)}) copy-start(s32[1024]{0:T(1024)S(1)} %pad_clamp_fusion) | copy-start | bytes 12292
  19.4 3.4 copy-start.11
  19.4 6.2 copy-start.10
  29.1 298.9 %all-reduce.2.cloned.1.call-start = ((), (), s32[]{:S(2)}) async-start(), calls=%async_computation.1 | async-start | bytes 14680064 | tf_op jit(solution)/shard_map/psum | solution.py:251
  29.2 37.8 %collective-permute-start.2 = (s32[512]{0:T(512)}, s32[512]{0:T(512)}, u32[]{:S(2)}, u32[]{:S(2)}) collective-permute-start(s32[512]{0:T(512)} %broadcast_add_fusion.3), channel_id=1, source_target_pairs={{0,16},{8,24},{16,32},{24,40},{32,48},{40,56},{48,64},{56,72},{64,... | collective-permute-start | bytes 6152 | tf_op jit(solution)/shard_map/ppermute | solution.py:21
  34.6 74.2 %collective-permute-start.4 = (bf16[512,448]{0,1:T(8,128)(2,1)}, bf16[512,448]{0,1:T(8,128)(2,1)}, u32[]{:S(2)}, u32[]{:S(2)}) collective-permute-start(bf16[512,448]{0,1:T(8,128)(2,1)} %param.25), channel_id=1, source_target_pairs={{0,16},{8,24},{16,32},{24,40},{32,48},{40,56},{48,64},{56,72},{64,... | collective-permute-start | bytes 1376264 | tf_op jit(solution)/shard_map/ppermute | solution.py:21
  38.7 70.1 %collective-permute-start.5 = (bf16[512,448]{0,1:T(8,128)(2,1)}, bf16[512,448]{0,1:T(8,128)(2,1)}, u32[]{:S(2)}, u32[]{:S(2)}) collective-permute-start(bf16[512,448]{0,1:T(8,128)(2,1)} %param.25), channel_id=1, source_target_pairs={{0,8},{8,16},{16,24},{24,32},{32,40},{40,48},{48,56},{56,64},{64,7... | collective-permute-start | bytes 1376264 | tf_op jit(solution)/shard_map/ppermute | solution.py:21
  43.0 68.3 %collective-permute-start = (bf16[512,448]{0,1:T(8,128)(2,1)}, bf16[512,448]{0,1:T(8,128)(2,1)}, u32[]{:S(2)}, u32[]{:S(2)}) collective-permute-start(bf16[512,448]{0,1:T(8,128)(2,1)} %param.26), channel_id=1, source_target_pairs={{0,16},{8,24},{16,32},{24,40},{32,48},{40,56},{48,64},{56,72},{64,... | collective-permute-start | bytes 1376264 | tf_op jit(solution)/shard_map/ppermute | solution.py:21
  47.0 64.3 %collective-permute-start.1 = (bf16[512,448]{0,1:T(8,128)(2,1)}, bf16[512,448]{0,1:T(8,128)(2,1)}, u32[]{:S(2)}, u32[]{:S(2)}) collective-permute-start(bf16[512,448]{0,1:T(8,128)(2,1)} %param.26), channel_id=1, source_target_pairs={{0,8},{8,16},{16,24},{24,32},{32,40},{40,48},{48,56},{56,64},{64,7... | collective-permute-start | bytes 1376264 | tf_op jit(solution)/shard_map/ppermute | solution.py:21
  56.1 13.5 %copy-start.15 = (f32[14]{0:T(128)S(1)}, f32[14]{0:T(128)}, u32[]{:S(2)}) copy-start(f32[14]{0:T(128)} %get-tuple-element.156) | copy-start | bytes 172
  66.9 44.3 %copy-start.6 = (bf16[512,448]{0,1:T(8,128)(2,1)S(1)}, bf16[512,448]{0,1:T(8,128)(2,1)}, u32[]{:S(2)}) copy-start(bf16[512,448]{0,1:T(8,128)(2,1)} %param.26) | copy-start | bytes 1376260
  167.6 2.3 copy-start.3
  167.6 2.3 copy-start.9
  167.6 2.4 copy-start.12
  167.6 2.4 copy-start.18
  213.5 4.2 copy-start.17
  217.8 8.2 %copy-start.8 = (bf16[2,224,512]{2,1,0:T(8,128)(2,1)S(1)}, bf16[2,224,512]{2,1,0:T(8,128)(2,1)}, u32[]{:S(2)}) copy-start(bf16[2,224,512]{2,1,0:T(8,128)(2,1)} %fusion.30) | copy-start | bytes 1376260
  226.0 5.2 copy-start.4
  228.2 3.0 copy-start.2
  237.4 154.6 %all-gather.7.cloned.1.call-start = ((), (), s32[]{:S(2)}) async-start(), calls=%async_computation.2 | async-start | bytes 6823936 | tf_op jit(solution)/shard_map/all_gather | solution.py:257
  238.1 217.5 %all-gather.11.cloned.1.call-start = ((), (), s32[]{:S(2)}) async-start(), calls=%async_computation.4 | async-start | bytes 6823936 | tf_op jit(solution)/shard_map/all_gather | solution.py:268
  238.7 280.5 %all-gather.9.cloned.1.call-start = ((), (), s32[]{:S(2)}) async-start(), calls=%async_computation.3 | async-start | bytes 6823936 | tf_op jit(solution)/shard_map/all_gather | solution.py:262
  239.3 152.7 %copy-start.16 = (f32[3584]{0:T(1024)S(1)}, f32[3584]{0:T(1024)}, u32[]{:S(2)}) copy-start(f32[3584]{0:T(1024)} %param.39) | copy-start | bytes 43012
  239.3 344.8 %reduce-scatter.4.cloned.1.call-start = ((), (), s32[]{:S(2)}) async-start(), calls=%async_computation.6 | async-start | bytes 8257536
  536.9 1.0 copy-start.5
  536.9 1.2 copy-start.7
  540.0 2.0 copy-start.19
  584.1 20.8 %copy-start.14 = (f32[448]{0:T(512)S(1)}, f32[448]{0:T(512)}, u32[]{:S(2)}) copy-start(f32[448]{0:T(512)} %param.43) | copy-start | bytes 5380
  584.1 24.8 %copy-start.1 = (bf16[448,3584]{1,0:T(8,128)(2,1)S(1)}, bf16[448,3584]{1,0:T(8,128)(2,1)}, u32[]{:S(2)}) copy-start(bf16[448,3584]{1,0:T(8,128)(2,1)} %param.37) | copy-start | bytes 9633796
Sparse Core Ops, SparseCore 0:
  29.2 88.2 all-gather.12
  237.5 90.5 all-reduce.1
  330.2 61.7 all-gather.6
  394.0 61.5 all-gather.10
  457.6 61.5 all-gather.8
  537.1 46.9 reduce-scatter.3
where the time goes:
time: 626 us; the launch traced here: 616 us
  waiting for transfers between devices  308 us (49%)
  matrix products  75 us (12%)
  blocking collectives  64.8 us (10%)
  other arithmetic  61.3 us (10%)
  local copies, waits for them, and re-layouts  55 us (9%)
  starting transfers between devices  25.2 us (4%)
  between operations  16.2 us (3%)
  loops' own time  11.1 us (2%)
    psum x1, waiting for transfers between devices, body(): lax.psum(lax.dynamic_update_slice_in_dim(projected, own_part, offset, 1),...  88.7 us
    all_gather x1, waiting for transfers between devices, body(): lax.all_gather(up_proj, 'req', axis=0, tiled=True)  63.6 us
    all_gather x1, waiting for transfers between devices, body(): lax.all_gather(gate_proj, 'req', axis=0, tiled=True)  60.3 us
    all_gather x1, waiting for transfers between devices, body(): lax.all_gather(down_proj, 'req', axis=1, tiled=True)  55.1 us
    unnamed x7, waiting for transfers between devices  39.8 us
    all_gather x1, blocking collectives, entering(): everything = jax.tree.map(lambda part: lax.all_gather(part, axis), x)  39.1 us
    select_n x16, other arithmetic, step(): return jax.tree.map(lambda a, b: jnp.where(reached, a, b), new, before)  32.6 us
    ppermute x6, starting transfers between devices, from_behind(): lax.ppermute(value, axis, [(source, source + steps) for source in range(l...  25 us
  transfers between devices with their start and end apart: 12, of which 5 were waited for; matrix products, arithmetic and copies ran while one was open for 10% of the time, Pallas kernels for 0%

commit v1 on v0

--- a/solution.py
+++ b/solution.py
@@ -13,6 +13,19 @@
 PAGE = 16
 EPSILON = 1e-05
 exact_mode = lax.Precision.HIGHEST
+
+
+def ring_gather(x, axis, dim):
+    ways = lax.axis_size(axis)
+    up = [(d, (d + 1) % ways) for d in range(ways)]
+    down = [(d, (d - 1) % ways) for d in range(ways)]
+    earlier, later = ([x], [x])
+    for _ in range(ways // 2):
+        earlier.append(lax.ppermute(earlier[-1], axis, up))
+    for _ in range((ways - 1) // 2):
+        later.append(lax.ppermute(later[-1], axis, down))
+    line = jnp.concatenate([*earlier[::-1], *later[1:]], axis=dim)
+    return jnp.roll(line, (lax.axis_index(axis) - ways // 2) * x.shape[dim], axis=dim)
 
 
 def from_behind(value, axis, steps):
@@ -257,11 +270,7 @@
         lax.all_gather(gate_proj, "req", axis=0, tiled=True),
         preferred_element_type=jnp.float32,
     )
-    up_act = jnp.dot(
-        normed,
-        lax.all_gather(up_proj, "req", axis=0, tiled=True),
-        preferred_element_type=jnp.float32,
-    )
+    up_act = jnp.dot(normed, ring_gather(up_proj, "req", 0), preferred_element_type=jnp.float32)
     latent_activation = (jax.nn.silu(gate_act) * up_act).astype(jnp.bfloat16)
     partial_value = jnp.dot(
         latent_activation,

time: 626 us -> 544 us (0.87)
  waiting for transfers between devices: 308 us -> 148 us
  local copies, waits for them, and re-layouts: 55 us -> 101 us
  starting transfers between devices: 25.2 us -> 65.5 us
  loops' own time: 11.1 us -> 0.5 us
    psum x1, waiting for transfers between devices: 88.7 us -> 0.01 us  [body(): lax.psum(lax.dynamic_update_slice_in_dim(projected, own_part, offset, 1),...]
    all_gather x1 -> x0, waiting for transfers between devices: 63.6 us -> none  [body(): lax.all_gather(up_proj, 'req', axis=0, tiled=True)]
    ppermute x0 -> x15, waiting for transfers between devices: none -> 59.1 us  [the longest x8 57.9 us: ring_gather(): earlier.append(lax.ppermute(earlier[-1], axis, up))]
    all_gather x1, waiting for transfers between devices: 60.3 us -> 12.8 us  [body(): lax.all_gather(gate_proj, 'req', axis=0, tiled=True)]
    ppermute x0 -> x15, starting transfers between devices: none -> 40.2 us  [the longest x7 38.4 us: ring_gather(): later.append(lax.ppermute(later[-1], axis, down))]
    unnamed x51 -> x94, local copies, waits for them, and re-layouts: 16.2 us -> 54 us
    another operation x1, loops' own time: 11.1 us -> 0.5 us  [entering(): return lax.fori_loop(0, devices, step, start)]
    all_gather x1, waiting for transfers between devices: 55.1 us -> 45.6 us  [body(): lax.all_gather(down_proj, 'req', axis=1, tiled=True)]
  transfers between devices with their start and end apart: 12 -> 26, of which waited for: 5 -> 13; matrix products, arithmetic and copies ran while one was open for 10% -> 22% of each run, Pallas kernels for 0% -> 0%
where the time goes in v1:
time: 544 us; the launch traced here: 534 us
  waiting for transfers between devices  148 us (27%)
  local copies, waits for them, and re-layouts  101 us (19%)
  matrix products  76.2 us (14%)
  starting transfers between devices  65.5 us (12%)
  blocking collectives  65 us (12%)
  other arithmetic  61.6 us (11%)
  between operations  15.8 us (3%)
    ppermute x8, waiting for transfers between devices, ring_gather(): earlier.append(lax.ppermute(earlier[-1], axis, up))  57.9 us
    unnamed x94, local copies, waits for them, and re-layouts  54 us
    all_gather x1, waiting for transfers between devices, body(): lax.all_gather(down_proj, 'req', axis=1, tiled=True)  45.6 us
    all_gather x1, blocking collectives, entering(): everything = jax.tree.map(lambda part: lax.all_gather(part, axis), x)  39.3 us
    ppermute x7, starting transfers between devices, ring_gather(): later.append(lax.ppermute(later[-1], axis, down))  38.4 us
    select_n x16, other arithmetic, step(): return jax.tree.map(lambda a, b: jnp.where(reached, a, b), new, before)  32.6 us
    unnamed x6, waiting for transfers between devices  30.3 us
    ppermute x6, starting transfers between devices, from_behind(): lax.ppermute(value, axis, [(source, source + steps) for source in range(l...  25.1 us
  transfers between devices with their start and end apart: 26, of which 13 were waited for; matrix products, arithmetic and copies ran while one was open for 22% of the time, Pallas kernels for 0%

profile of v1, /device:TPU:0, one launch (start us, length us, event | category | flops | bytes accessed | tf_op | source)
XLA Modules:
  0.0 533.8 jit_solution(1826448649908160974)
XLA Ops:
  8.7 3.6 collective-permute-start.3
  16.9 2.5 copy.75
  25.6 3.5 fusion.24
  29.2 5.3 %collective-permute-start.2 = (s32[512]{0:T(512)}, s32[512]{0:T(512)}, u32[]{:S(2)}, u32[]{:S(2)}) collective-permute-start(s32[512]{0:T(512)} %broadcast_add_fusion.3), channel_id=1, source_target_pairs={{0,16},{8,24},{16,32},{24,40},{32,48},{40,56},{48,64},{56,72},{64,... | collective-permute-start | bytes 6152 | tf_op jit(solution)/shard_map/ppermute | solution.py:34
  34.5 4.1 collective-permute-start.4
  38.7 4.2 collective-permute-start.5
  42.9 4.1 collective-permute-start
  47.0 3.7 collective-permute-start.1
  56.1 8.7 %gather_fusion = f32[14,512,512]{2,1,0:T(8,128)} fusion(f32[2,512,512]{2,1,0:T(8,128)} %fusion.63, s32[1024]{0:T(1024)} %copy-done.19), kind=kCustom, calls=%fused_computation | custom fusion | bytes 29360184 | tf_op jit(solution)/shard_map/gather | solution.py:98
  69.4 39.3 %all-gather.1 = f32[16,1,14]{2,1,0:T(1,128)S(1)} all-gather(f32[1,1,14]{2,1,0:T(1,128)S(1)} %bitcast.114), channel_id=1, replica_groups=mesh['req'=16,'mlp'=8] {'req'}, dimensions={0}, use_global_device_ids=true | all-gather | bytes 952 | tf_op jit(solution)/shard_map/all_gather | solution.py:39
  108.7 2.5 pad_maximum_fusion.1
  111.3 2.5 pad_maximum_fusion
  113.8 4.1 fusion.62
  117.9 6.2 %fusion.34 = bf16[2,224,512]{2,1,0:T(8,128)(2,1)} fusion(bf16[1536,2,224]{0,2,1:T(8,128)(2,1)} %bitcast.105, f32[2,512]{1,0:T(2,128)S(1)} %fusion.62, pred[512,1536]{0,1:T(8,128)(4,1)} %compare_and_fusion, bf16[1536,2,224]{0,2,1:T(8,128)(2,1)} %bitcast.104, bf16[512,2,224]{0,2,1:T(8,128)(2,1)} %bitcast.116), kind=kOutput, calls=%fused_computation.51 | convolution fusion | flops 1417382400 | bytes 4460544 | tf_op jit(solution)/shard_map/while/body/eval_jaxpr/hqk,khd->qhd/dot_general | solution.py:68
  124.1 33.2 %while.18 = (s32[]{:T(128)}, f32[14,64,64]{2,1,0:T(8,128)}, s32[]{:T(128)}, f32[16,14]{1,0:T(8,128)S(1)}, f32[16,14,64,64]{3,2,1,0:T(8,128)}, /*index=5*/s32[]{:T(128)}, s32[]{:T(128)}) while((s32[]{:T(128)}, f32[14,64,64]{2,1,0:T(8,128)}, s32[]{:T(128)}, f32[16,14]{1,0:T(8,128)S(1)}, f32[16,14,64,64]{3,2,1,0:T(8,128)}, ...), condition=%wide.region_5.6_spmd.clone, body=%wide.region_4.5_spmd.clone.sunk | while | flops 229380 | bytes 688401 | solution.py:49
  126.6 2.0 fusion.79
  128.6 2.0 fusion.79
  130.7 2.0 fusion.79
  138.9 2.0 fusion.79
  140.9 2.0 fusion.79
  143.0 2.0 fusion.79
  145.0 2.0 fusion.79
  147.1 2.0 fusion.79
  149.1 2.1 fusion.79
  153.2 2.0 fusion.79
  155.3 2.0 fusion.79
  157.3 2.2 fusion.41
  159.5 21.0 %fusion.23 = f32[512,14,64]{0,2,1:T(8,128)} fusion(f32[14,512,64]{1,2,0:T(8,128)S(1)} %fusion.41, f32[512,14,64]{0,2,1:T(8,128)} %bitcast.98, f32[14,512,512]{2,1,0:T(8,128)} %gather_fusion, f32[14,512]{1,0:T(8,128)S(1)} %bitcast.111, pred[512,512]{1,0:T(8,128)(4,1)S(1)} %copy-done.16, f32[14]{0:T(128)S(1)} %copy-done.24, ...), kind=kOutput, calls=%fused_computation.40 | convolution fusion | flops 2831876096 | bytes 20533304 | tf_op jit(solution)/shard_map/htu,uhp->thp/dot_general | solution.py:97
  180.6 2.8 copy.80
  183.3 3.5 fusion.60
  186.8 2.8 copy.81
  191.2 12.4 %psum.21 = f32[512,2]{0,1:T(2,128)S(1)} all-reduce(f32[512,2]{0,1:T(2,128)S(1)} %reduce_sum.38), channel_id=1, replica_groups=mesh['req'=16,'mlp'=8] {'mlp'}, use_global_device_ids=true, to_apply=%region_7.8 | all-reduce | flops 1024 | bytes 8192 | tf_op jit(solution)/shard_map/psum | solution.py:248
  205.1 2.9 copy.82
  208.1 8.2 %fusion.39 = f32[512,3584]{1,0:T(8,128)S(1)} fusion(bf16[896,3584]{1,0:T(8,128)(2,1)} %param.38, f32[512,896]{1,0:T(8,128)} %copy.82, f32[896]{0:T(1024)S(1)} %copy-done.23, f32[512,896]{1,0:T(8,128)} %copy.80, bf16[512,896]{1,0:T(8,128)(2,1)} %param.30), kind=kOutput, calls=%fused_computation.59 | convolution fusion | flops 3292463104 | bytes 18353664 | tf_op jit(solution)/shard_map/dot_general | solution.py:256
  216.3 2.2 convolution_add_fusion
  218.5 3.0 copy-done.2
  221.9 5.8 %dynamic_update_slice.6 = f32[512,3584]{1,0:T(8,128)} dynamic-update-slice(f32[512,3584]{1,0:T(8,128)} %copy-done.2, f32[512,448]{1,0:T(8,128)S(1)} %convert_add_fusion, s32[]{:T(128)} %constant.119.clone.1, s32[]{:T(128)S(6)} %select_n.116) | dynamic-update-slice | bytes 1835012 | tf_op jit(solution)/shard_map/dynamic_update_slice | solution.py:264
  230.9 13.2 %collective-permute-done.6 = bf16[224,896]{1,0:T(8,128)(2,1)S(1)} collective-permute-done((bf16[224,896]{1,0:T(8,128)(2,1)S(1)}, bf16[224,896]{1,0:T(8,128)(2,1)S(1)}, u32[]{:S(2)}, u32[]{:S(2)}) %collective-permute-start.6) | collective-permute-done | bytes 401440 | tf_op jit(solution)/shard_map/ppermute | solution.py:24
  244.1 5.3 %collective-permute-start.14 = (bf16[224,896]{1,0:T(8,128)(2,1)S(1)}, bf16[224,896]{1,0:T(8,128)(2,1)S(1)}, u32[]{:S(2)}, u32[]{:S(2)}) collective-permute-start(bf16[224,896]{1,0:T(8,128)(2,1)S(1)} %copy-done.6), channel_id=1, source_target_pairs={{0,120},{8,0},{16,8},{24,16},{32,24},{40,32},{48,40},{56,48},{64,5... | collective-permute-start | bytes 1204232 | tf_op jit(solution)/shard_map/ppermute | solution.py:26
  249.5 8.8 %collective-permute-done.7 = bf16[224,896]{1,0:T(8,128)(2,1)S(1)} collective-permute-done((bf16[224,896]{1,0:T(8,128)(2,1)S(1)}, bf16[224,896]{1,0:T(8,128)(2,1)S(1)}, u32[]{:S(2)}, u32[]{:S(2)}) %collective-permute-start.7) | collective-permute-done | bytes 401440 | tf_op jit(solution)/shard_map/ppermute | solution.py:24
  258.3 5.3 %collective-permute-start.15 = (bf16[224,896]{1,0:T(8,128)(2,1)S(1)}, bf16[224,896]{1,0:T(8,128)(2,1)S(1)}, u32[]{:S(2)}, u32[]{:S(2)}) collective-permute-start(bf16[224,896]{1,0:T(8,128)(2,1)S(1)} %collective-permute-done.14), channel_id=1, source_target_pairs={{0,120},{8,0},{16,8},{24,16},{32,24},{40,32},{48,40},{56,48},{64,5... | collective-permute-start | bytes 1204232 | tf_op jit(solution)/shard_map/ppermute | solution.py:26
  263.6 7.9 %collective-permute-done.8 = bf16[224,896]{1,0:T(8,128)(2,1)S(1)} collective-permute-done((bf16[224,896]{1,0:T(8,128)(2,1)S(1)}, bf16[224,896]{1,0:T(8,128)(2,1)S(1)}, u32[]{:S(2)}, u32[]{:S(2)}) %collective-permute-start.8) | collective-permute-done | bytes 401440 | tf_op jit(solution)/shard_map/ppermute | solution.py:24
  271.5 5.3 %collective-permute-start.16 = (bf16[224,896]{1,0:T(8,128)(2,1)S(1)}, bf16[224,896]{1,0:T(8,128)(2,1)S(1)}, u32[]{:S(2)}, u32[]{:S(2)}) collective-permute-start(bf16[224,896]{1,0:T(8,128)(2,1)S(1)} %collective-permute-done.15), channel_id=1, source_target_pairs={{0,120},{8,0},{16,8},{24,16},{32,24},{40,32},{48,40},{56,48},{64,5... | collective-permute-start | bytes 1204232 | tf_op jit(solution)/shard_map/ppermute | solution.py:26
  276.9 7.0 %collective-permute-done.9 = bf16[224,896]{1,0:T(8,128)(2,1)S(1)} collective-permute-done((bf16[224,896]{1,0:T(8,128)(2,1)S(1)}, bf16[224,896]{1,0:T(8,128)(2,1)S(1)}, u32[]{:S(2)}, u32[]{:S(2)}) %collective-permute-start.9) | collective-permute-done | bytes 401440 | tf_op jit(solution)/shard_map/ppermute | solution.py:24
  283.9 5.3 %collective-permute-start.17 = (bf16[224,896]{1,0:T(8,128)(2,1)S(1)}, bf16[224,896]{1,0:T(8,128)(2,1)S(1)}, u32[]{:S(2)}, u32[]{:S(2)}) collective-permute-start(bf16[224,896]{1,0:T(8,128)(2,1)S(1)} %collective-permute-done.16), channel_id=1, source_target_pairs={{0,120},{8,0},{16,8},{24,16},{32,24},{40,32},{48,40},{56,48},{64,5... | collective-permute-start | bytes 1204232 | tf_op jit(solution)/shard_map/ppermute | solution.py:26
  289.2 6.1 %collective-permute-done.10 = bf16[224,896]{1,0:T(8,128)(2,1)S(1)} collective-permute-done((bf16[224,896]{1,0:T(8,128)(2,1)S(1)}, bf16[224,896]{1,0:T(8,128)(2,1)S(1)}, u32[]{:S(2)}, u32[]{:S(2)}) %collective-permute-start.10) | collective-permute-done | bytes 401440 | tf_op jit(solution)/shard_map/ppermute | solution.py:24
  296.1 5.3 collective-permute-start.18
  301.4 5.1 collective-permute-done.11
  306.8 5.9 %collective-permute-start.19 = (bf16[224,896]{1,0:T(8,128)(2,1)}, bf16[224,896]{1,0:T(8,128)(2,1)}, u32[]{:S(2)}, u32[]{:S(2)}) collective-permute-start(bf16[224,896]{1,0:T(8,128)(2,1)} %collective-permute-done.18), channel_id=1, source_target_pairs={{0,120},{8,0},{16,8},{24,16},{32,24},{40,32},{48,40},{56,48},{64,5... | collective-permute-start | bytes 1204232 | tf_op jit(solution)/shard_map/ppermute | solution.py:26
  312.7 5.1 collective-permute-done.12
  318.7 5.8 %collective-permute-start.20 = (bf16[224,896]{1,0:T(8,128)(2,1)}, bf16[224,896]{1,0:T(8,128)(2,1)S(1)}, u32[]{:S(2)}, u32[]{:S(2)}) collective-permute-start(bf16[224,896]{1,0:T(8,128)(2,1)} %collective-permute-done.19), channel_id=1, source_target_pairs={{0,120},{8,0},{16,8},{24,16},{32,24},{40,32},{48,40},{56,48},{64,5... | collective-permute-start | bytes 1204232 | tf_op jit(solution)/shard_map/ppermute | solution.py:26
  324.5 4.8 collective-permute-done.13
  366.0 3.8 multiply_reduce_fusion
  369.8 12.8 %all-gather.6.cloned.1.call-done = bf16[3584,896]{1,0:T(8,128)(2,1)} async-done(((bf16[224,896]{1,0:T(8,128)(2,1)}), bf16[3584,896]{1,0:T(8,128)(2,1)}) %all-gather.6.cloned.1.call-update) | async-done | bytes 6422544 | tf_op jit(solution)/shard_map/all_gather | solution.py:270
  382.6 8.5 %fusion.61 = f32[512,896]{1,0:T(8,128)S(1)} fusion(bf16[3584,896]{1,0:T(8,128)(2,1)} %all-gather.6.cloned.1.call-done, f32[512,3584]{1,0:T(8,128)} %all-reduce.2.cloned.1.call-done, f32[3584]{0:T(1024)S(1)} %copy-done.22, f32[512]{0:T(512)S(1)} %add_rsqrt_fusion.2), kind=kOutput, calls=%fused_computation.132 | convolution fusion | flops 3293839360 | bytes 15613952 | tf_op jit(solution)/shard_map/dot_general | solution.py:268
  391.0 9.5 %multiply_convert_fusion.1 = bf16[512,896]{1,0:T(8,128)(2,1)S(1)} fusion(f32[512,896]{1,0:T(8,128)S(1)} %fusion.61, bf16[7168,896]{1,0:T(8,128)(2,1)} %constant_dynamic-update-slice_fusion, s32[]{:T(128)S(6)} %select_n.118, f32[512,3584]{1,0:T(8,128)} %all-reduce.2.cloned.1.call-done, f32[3584]{0:T(1024)S(1)} %copy-done.22, f32[512]{0:T(512)S(1)} %add_rsqrt_fusion.2), kind=kOutput, calls=%fused_computation.41 | convolution fusion | flops 3296591872 | bytes 16531460 | tf_op jit(solution)/shard_map/dot_general | solution.py:273
  400.6 45.6 %all-gather.8.cloned.1.call-done = bf16[896,3584]{0,1:T(8,128)(2,1)} async-done(((bf16[896,224]{0,1:T(8,128)(2,1)}), bf16[896,3584]{0,1:T(8,128)(2,1)}) %all-gather.8.cloned.1.call-update) | async-done | bytes 6422544 | tf_op jit(solution)/shard_map/all_gather | solution.py:277
  446.1 8.9 %convolution_bitcast_fusion = f32[3584,512]{1,0:T(8,128)} fusion(bf16[512,896]{1,0:T(8,128)(2,1)S(1)} %multiply_convert_fusion.1, bf16[896,3584]{0,1:T(8,128)(2,1)} %all-gather.8.cloned.1.call-done), kind=kOutput, calls=%fused_computation.19 | convolution fusion | flops 3288334336 | bytes 14680064
  462.4 8.5 %scatter_fusion = bf16[2,2,32,3584]{3,1,2,0:T(2,128)(2,1)} fusion(bf16[2,2,32,3584]{3,1,2,0:T(2,128)(2,1)} %broadcast_in_dim.106, s32[32]{0:T(128)S(1)} %fusion.51, bf16[32,2,2,3584]{3,2,1,0:T(2,128)(2,1)} %copy.89), kind=kCustom, calls=%fused_computation.3 | custom fusion | bytes 2752640 | tf_op jit(solution)/shard_map/scatter | solution.py:210
  471.0 2.2 copy.92
  473.2 29.0 %reduce-scatter.4.cloned.1.call-done = f32[448,512]{1,0:T(8,128)} async-done(((f32[3584,512]{1,0:T(8,128)}), f32[448,512]{1,0:T(8,128)}) %reduce-scatter.4.cloned.1.call-update) | async-done | bytes 917520
  502.2 2.6 copy.96
  504.8 2.8 fusion.35
  507.6 13.2 %psum.23 = f32[512]{0:T(512)S(1)} all-reduce(f32[512]{0:T(512)S(1)} %get-tuple-element.167), channel_id=1, replica_groups=mesh['req'=16,'mlp'=8] {'mlp'}, use_global_device_ids=true, to_apply=%region_12.13 | all-reduce | flops 512 | bytes 4096 | tf_op jit(solution)/shard_map/psum | solution.py:283
  (191 shorter events, 89.9 us)
Async XLA Ops:
  7.2 209.1 %copy-start = (bf16[448,3584]{1,0:T(8,128)(2,1)S(1)}, bf16[448,3584]{1,0:T(8,128)(2,1)}, u32[]{:S(2)}) copy-start(bf16[448,3584]{1,0:T(8,128)(2,1)} %param.37) | copy-start | bytes 9633796
  7.2 15.7 %copy-start.18 = (s32[512]{0:T(512)S(1)}, s32[512]{0:T(512)}, u32[]{:S(2)}) copy-start(s32[512]{0:T(512)} %param.27) | copy-start | bytes 6148
  7.2 18.4 %copy-start.17 = (f32[512,14]{0,1:T(8,128)S(1)}, f32[512,14]{0,1:T(8,128)}, u32[]{:S(2)}) copy-start(f32[512,14]{0,1:T(8,128)} %param.33) | copy-start | bytes 86020
  7.2 116.9 %all-gather.10.cloned.1.call-start = ((), (), s32[]{:S(2)}) async-start(), calls=%async_computation.4 | async-start | bytes 7798784 | tf_op jit(solution)/shard_map/all_gather | solution.py:39
  8.7 12.3 %collective-permute-start.3 = (s32[512]{0:T(512)}, s32[512]{0:T(512)S(1)}, u32[]{:S(2)}, u32[]{:S(2)}) collective-permute-start(s32[512]{0:T(512)} %broadcast_add_fusion.3), channel_id=1, source_target_pairs={{0,8},{8,16},{16,24},{24,32},{32,40},{40,48},{48,56},{56,64},{64,7... | collective-permute-start | bytes 6152 | tf_op jit(solution)/shard_map/ppermute | solution.py:34
  14.6 10.4 %copy-start.19 = (s32[1024]{0:T(1024)}, s32[1024]{0:T(1024)S(1)}, u32[]{:S(2)}) copy-start(s32[1024]{0:T(1024)S(1)} %pad_clamp_fusion) | copy-start | bytes 12292
  29.1 336.8 %all-reduce.2.cloned.1.call-start = ((), (), s32[]{:S(2)}) async-start(), calls=%async_computation.1 | async-start | bytes 14680064 | tf_op jit(solution)/shard_map/psum | solution.py:264
  29.2 37.7 %collective-permute-start.2 = (s32[512]{0:T(512)}, s32[512]{0:T(512)}, u32[]{:S(2)}, u32[]{:S(2)}) collective-permute-start(s32[512]{0:T(512)} %broadcast_add_fusion.3), channel_id=1, source_target_pairs={{0,16},{8,24},{16,32},{24,40},{32,48},{40,56},{48,64},{56,72},{64,... | collective-permute-start | bytes 6152 | tf_op jit(solution)/shard_map/ppermute | solution.py:34
  34.5 74.2 %collective-permute-start.4 = (bf16[512,448]{0,1:T(8,128)(2,1)}, bf16[512,448]{0,1:T(8,128)(2,1)}, u32[]{:S(2)}, u32[]{:S(2)}) collective-permute-start(bf16[512,448]{0,1:T(8,128)(2,1)} %param.25), channel_id=1, source_target_pairs={{0,16},{8,24},{16,32},{24,40},{32,48},{40,56},{48,64},{56,72},{64,... | collective-permute-start | bytes 1376264 | tf_op jit(solution)/shard_map/ppermute | solution.py:34
  38.7 70.1 %collective-permute-start.5 = (bf16[512,448]{0,1:T(8,128)(2,1)}, bf16[512,448]{0,1:T(8,128)(2,1)}, u32[]{:S(2)}, u32[]{:S(2)}) collective-permute-start(bf16[512,448]{0,1:T(8,128)(2,1)} %param.25), channel_id=1, source_target_pairs={{0,8},{8,16},{16,24},{24,32},{32,40},{40,48},{48,56},{56,64},{64,7... | collective-permute-start | bytes 1376264 | tf_op jit(solution)/shard_map/ppermute | solution.py:34
  42.9 68.4 %collective-permute-start = (bf16[512,448]{0,1:T(8,128)(2,1)}, bf16[512,448]{0,1:T(8,128)(2,1)}, u32[]{:S(2)}, u32[]{:S(2)}) collective-permute-start(bf16[512,448]{0,1:T(8,128)(2,1)} %param.26), channel_id=1, source_target_pairs={{0,16},{8,24},{16,32},{24,40},{32,48},{40,56},{48,64},{56,72},{64,... | collective-permute-start | bytes 1376264 | tf_op jit(solution)/shard_map/ppermute | solution.py:34
  47.0 64.3 %collective-permute-start.1 = (bf16[512,448]{0,1:T(8,128)(2,1)}, bf16[512,448]{0,1:T(8,128)(2,1)}, u32[]{:S(2)}, u32[]{:S(2)}) collective-permute-start(bf16[512,448]{0,1:T(8,128)(2,1)} %param.26), channel_id=1, source_target_pairs={{0,8},{8,16},{16,24},{24,32},{32,40},{40,48},{48,56},{56,64},{64,7... | collective-permute-start | bytes 1376264 | tf_op jit(solution)/shard_map/ppermute | solution.py:34
  56.1 13.3 %copy-start.21 = (f32[14]{0:T(128)S(1)}, f32[14]{0:T(128)}, u32[]{:S(2)}) copy-start(f32[14]{0:T(128)} %get-tuple-element.156) | copy-start | bytes 172
  124.1 35.4 %copy-start.16 = (pred[512,512]{1,0:T(8,128)(4,1)S(1)}, pred[512,512]{1,0:T(8,128)(4,1)}, u32[]{:S(2)}) copy-start(pred[512,512]{1,0:T(8,128)(4,1)} %fusion.38) | copy-start | bytes 786436
  124.1 35.4 %copy-start.24 = (f32[14]{0:T(128)S(1)}, f32[14]{0:T(128)}, u32[]{:S(2)}) copy-start(f32[14]{0:T(128)} %param.35) | copy-start | bytes 172
  186.8 21.2 %copy-start.23 = (f32[896]{0:T(1024)S(1)}, f32[896]{0:T(1024)}, u32[]{:S(2)}) copy-start(f32[896]{0:T(1024)} %param.36) | copy-start | bytes 10756
  208.1 8.2 %copy-start.15 = (bf16[2,224,512]{2,1,0:T(8,128)(2,1)S(1)}, bf16[2,224,512]{2,1,0:T(8,128)(2,1)}, u32[]{:S(2)}) copy-start(bf16[2,224,512]{2,1,0:T(8,128)(2,1)} %fusion.34) | copy-start | bytes 1376260
  216.3 5.2 copy-start.3
  218.5 3.0 copy-start.2
  221.5 7.6 %copy-start.6 = (bf16[224,896]{1,0:T(8,128)(2,1)S(1)}, bf16[224,896]{1,0:T(8,128)(2,1)}, u32[]{:S(2)}) copy-start(bf16[224,896]{1,0:T(8,128)(2,1)} %param.41) | copy-start | bytes 1204228
  227.7 154.8 %all-gather.6.cloned.1.call-start = ((), (), s32[]{:S(2)}) async-start(), calls=%async_computation.2 | async-start | bytes 6823936 | tf_op jit(solution)/shard_map/all_gather | solution.py:270
  228.5 217.7 %all-gather.8.cloned.1.call-start = ((), (), s32[]{:S(2)}) async-start(), calls=%async_computation.3 | async-start | bytes 6823936 | tf_op jit(solution)/shard_map/all_gather | solution.py:277
  229.1 273.2 %reduce-scatter.4.cloned.1.call-start = ((), (), s32[]{:S(2)}) async-start(), calls=%async_computation.5 | async-start | bytes 8257536
  229.1 15.0 %collective-permute-start.6 = (bf16[224,896]{1,0:T(8,128)(2,1)S(1)}, bf16[224,896]{1,0:T(8,128)(2,1)S(1)}, u32[]{:S(2)}, u32[]{:S(2)}) collective-permute-start(bf16[224,896]{1,0:T(8,128)(2,1)S(1)} %copy-done.6), channel_id=1, source_target_pairs={{0,8},{8,16},{16,24},{24,32},{32,40},{40,48},{48,56},{56,64},{64,7... | collective-permute-start | bytes 1204232 | tf_op jit(solution)/shard_map/ppermute | solution.py:24
  244.1 14.2 %collective-permute-start.7 = (bf16[224,896]{1,0:T(8,128)(2,1)S(1)}, bf16[224,896]{1,0:T(8,128)(2,1)S(1)}, u32[]{:S(2)}, u32[]{:S(2)}) collective-permute-start(bf16[224,896]{1,0:T(8,128)(2,1)S(1)} %collective-permute-done.6), channel_id=1, source_target_pairs={{0,8},{8,16},{16,24},{24,32},{32,40},{40,48},{48,56},{56,64},{64,7... | collective-permute-start | bytes 1204232 | tf_op jit(solution)/shard_map/ppermute | solution.py:24
  244.1 14.2 %collective-permute-start.14 = (bf16[224,896]{1,0:T(8,128)(2,1)S(1)}, bf16[224,896]{1,0:T(8,128)(2,1)S(1)}, u32[]{:S(2)}, u32[]{:S(2)}) collective-permute-start(bf16[224,896]{1,0:T(8,128)(2,1)S(1)} %copy-done.6), channel_id=1, source_target_pairs={{0,120},{8,0},{16,8},{24,16},{32,24},{40,32},{48,40},{56,48},{64,5... | collective-permute-start | bytes 1204232 | tf_op jit(solution)/shard_map/ppermute | solution.py:26
  258.3 13.3 %collective-permute-start.8 = (bf16[224,896]{1,0:T(8,128)(2,1)S(1)}, bf16[224,896]{1,0:T(8,128)(2,1)S(1)}, u32[]{:S(2)}, u32[]{:S(2)}) collective-permute-start(bf16[224,896]{1,0:T(8,128)(2,1)S(1)} %collective-permute-done.7), channel_id=1, source_target_pairs={{0,8},{8,16},{16,24},{24,32},{32,40},{40,48},{48,56},{56,64},{64,7... | collective-permute-start | bytes 1204232 | tf_op jit(solution)/shard_map/ppermute | solution.py:24
  258.3 13.3 %collective-permute-start.15 = (bf16[224,896]{1,0:T(8,128)(2,1)S(1)}, bf16[224,896]{1,0:T(8,128)(2,1)S(1)}, u32[]{:S(2)}, u32[]{:S(2)}) collective-permute-start(bf16[224,896]{1,0:T(8,128)(2,1)S(1)} %collective-permute-done.14), channel_id=1, source_target_pairs={{0,120},{8,0},{16,8},{24,16},{32,24},{40,32},{48,40},{56,48},{64,5... | collective-permute-start | bytes 1204232 | tf_op jit(solution)/shard_map/ppermute | solution.py:26
  271.5 12.3 %collective-permute-start.9 = (bf16[224,896]{1,0:T(8,128)(2,1)S(1)}, bf16[224,896]{1,0:T(8,128)(2,1)S(1)}, u32[]{:S(2)}, u32[]{:S(2)}) collective-permute-start(bf16[224,896]{1,0:T(8,128)(2,1)S(1)} %collective-permute-done.8), channel_id=1, source_target_pairs={{0,8},{8,16},{16,24},{24,32},{32,40},{40,48},{48,56},{56,64},{64,7... | collective-permute-start | bytes 1204232 | tf_op jit(solution)/shard_map/ppermute | solution.py:24
  271.5 12.3 %collective-permute-start.16 = (bf16[224,896]{1,0:T(8,128)(2,1)S(1)}, bf16[224,896]{1,0:T(8,128)(2,1)S(1)}, u32[]{:S(2)}, u32[]{:S(2)}) collective-permute-start(bf16[224,896]{1,0:T(8,128)(2,1)S(1)} %collective-permute-done.15), channel_id=1, source_target_pairs={{0,120},{8,0},{16,8},{24,16},{32,24},{40,32},{48,40},{56,48},{64,5... | collective-permute-start | bytes 1204232 | tf_op jit(solution)/shard_map/ppermute | solution.py:26
  283.9 22.9 %copy-start.9 = (bf16[224,896]{1,0:T(8,128)(2,1)}, bf16[224,896]{1,0:T(8,128)(2,1)S(1)}, u32[]{:S(2)}) copy-start(bf16[224,896]{1,0:T(8,128)(2,1)S(1)} %collective-permute-done.9) | copy-start | bytes 1204228
  283.9 11.4 %collective-permute-start.10 = (bf16[224,896]{1,0:T(8,128)(2,1)S(1)}, bf16[224,896]{1,0:T(8,128)(2,1)S(1)}, u32[]{:S(2)}, u32[]{:S(2)}) collective-permute-start(bf16[224,896]{1,0:T(8,128)(2,1)S(1)} %collective-permute-done.9), channel_id=1, source_target_pairs={{0,8},{8,16},{16,24},{24,32},{32,40},{40,48},{48,56},{56,64},{64,7... | collective-permute-start | bytes 1204232 | tf_op jit(solution)/shard_map/ppermute | solution.py:24
  283.9 11.4 %collective-permute-start.17 = (bf16[224,896]{1,0:T(8,128)(2,1)S(1)}, bf16[224,896]{1,0:T(8,128)(2,1)S(1)}, u32[]{:S(2)}, u32[]{:S(2)}) collective-permute-start(bf16[224,896]{1,0:T(8,128)(2,1)S(1)} %collective-permute-done.16), channel_id=1, source_target_pairs={{0,120},{8,0},{16,8},{24,16},{32,24},{40,32},{48,40},{56,48},{64,5... | collective-permute-start | bytes 1204232 | tf_op jit(solution)/shard_map/ppermute | solution.py:26
  295.3 17.4 %copy-start.11 = (bf16[224,896]{1,0:T(8,128)(2,1)}, bf16[224,896]{1,0:T(8,128)(2,1)S(1)}, u32[]{:S(2)}) copy-start(bf16[224,896]{1,0:T(8,128)(2,1)S(1)} %collective-permute-done.10) | copy-start | bytes 1204228
  295.3 11.2 %collective-permute-start.11 = (bf16[224,896]{1,0:T(8,128)(2,1)S(1)}, bf16[224,896]{1,0:T(8,128)(2,1)S(1)}, u32[]{:S(2)}, u32[]{:S(2)}) collective-permute-start(bf16[224,896]{1,0:T(8,128)(2,1)S(1)} %collective-permute-done.10), channel_id=1, source_target_pairs={{0,8},{8,16},{16,24},{24,32},{32,40},{40,48},{48,56},{56,64},{64,7... | collective-permute-start | bytes 1204232 | tf_op jit(solution)/shard_map/ppermute | solution.py:24
  295.3 0.8 copy-start.7
  296.1 10.7 %collective-permute-start.18 = (bf16[224,896]{1,0:T(8,128)(2,1)S(1)}, bf16[224,896]{1,0:T(8,128)(2,1)}, u32[]{:S(2)}, u32[]{:S(2)}) collective-permute-start(bf16[224,896]{1,0:T(8,128)(2,1)S(1)} %collective-permute-done.17), channel_id=1, source_target_pairs={{0,120},{8,0},{16,8},{24,16},{32,24},{40,32},{48,40},{56,48},{64,5... | collective-permute-start | bytes 1204232 | tf_op jit(solution)/shard_map/ppermute | solution.py:26
  306.5 11.3 %copy-start.13 = (bf16[224,896]{1,0:T(8,128)(2,1)}, bf16[224,896]{1,0:T(8,128)(2,1)S(1)}, u32[]{:S(2)}) copy-start(bf16[224,896]{1,0:T(8,128)(2,1)S(1)} %collective-permute-done.11) | copy-start | bytes 1204228
  306.5 11.3 %collective-permute-start.12 = (bf16[224,896]{1,0:T(8,128)(2,1)S(1)}, bf16[224,896]{1,0:T(8,128)(2,1)}, u32[]{:S(2)}, u32[]{:S(2)}) collective-permute-start(bf16[224,896]{1,0:T(8,128)(2,1)S(1)} %collective-permute-done.11), channel_id=1, source_target_pairs={{0,8},{8,16},{16,24},{24,32},{32,40},{40,48},{48,56},{56,64},{64,7... | collective-permute-start | bytes 1204232 | tf_op jit(solution)/shard_map/ppermute | solution.py:24
  306.8 11.9 %collective-permute-start.19 = (bf16[224,896]{1,0:T(8,128)(2,1)}, bf16[224,896]{1,0:T(8,128)(2,1)}, u32[]{:S(2)}, u32[]{:S(2)}) collective-permute-start(bf16[224,896]{1,0:T(8,128)(2,1)} %collective-permute-done.18), channel_id=1, source_target_pairs={{0,120},{8,0},{16,8},{24,16},{32,24},{40,32},{48,40},{56,48},{64,5... | collective-permute-start | bytes 1204232 | tf_op jit(solution)/shard_map/ppermute | solution.py:26
  317.8 11.5 %collective-permute-start.13 = (bf16[224,896]{1,0:T(8,128)(2,1)}, bf16[224,896]{1,0:T(8,128)(2,1)}, u32[]{:S(2)}, u32[]{:S(2)}) collective-permute-start(bf16[224,896]{1,0:T(8,128)(2,1)} %collective-permute-done.12), channel_id=1, source_target_pairs={{0,8},{8,16},{16,24},{24,32},{32,40},{40,48},{48,56},{56,64},{64,7... | collective-permute-start | bytes 1204232 | tf_op jit(solution)/shard_map/ppermute | solution.py:24
  317.8 26.4 %copy-start.8 = (bf16[224,896]{1,0:T(8,128)(2,1)S(1)}, bf16[224,896]{1,0:T(8,128)(2,1)}, u32[]{:S(2)}) copy-start(bf16[224,896]{1,0:T(8,128)(2,1)} %copy-done.7) | copy-start | bytes 1204228
  318.7 29.8 %collective-permute-start.20 = (bf16[224,896]{1,0:T(8,128)(2,1)}, bf16[224,896]{1,0:T(8,128)(2,1)S(1)}, u32[]{:S(2)}, u32[]{:S(2)}) collective-permute-start(bf16[224,896]{1,0:T(8,128)(2,1)} %collective-permute-done.19), channel_id=1, source_target_pairs={{0,120},{8,0},{16,8},{24,16},{32,24},{40,32},{48,40},{56,48},{64,5... | collective-permute-start | bytes 1204232 | tf_op jit(solution)/shard_map/ppermute | solution.py:26
  332.9 19.9 %copy-start.14 = (bf16[224,896]{1,0:T(8,128)(2,1)S(1)}, bf16[224,896]{1,0:T(8,128)(2,1)}, u32[]{:S(2)}) copy-start(bf16[224,896]{1,0:T(8,128)(2,1)} %copy-done.13) | copy-start | bytes 1204228
  334.8 18.9 %copy-start.12 = (bf16[224,896]{1,0:T(8,128)(2,1)S(1)}, bf16[224,896]{1,0:T(8,128)(2,1)}, u32[]{:S(2)}) copy-start(bf16[224,896]{1,0:T(8,128)(2,1)} %copy-done.11) | copy-start | bytes 1204228
  336.7 17.8 %copy-start.10 = (bf16[224,896]{1,0:T(8,128)(2,1)S(1)}, bf16[224,896]{1,0:T(8,128)(2,1)}, u32[]{:S(2)}) copy-start(bf16[224,896]{1,0:T(8,128)(2,1)} %copy-done.9) | copy-start | bytes 1204228
  358.4 24.1 %copy-start.22 = (f32[3584]{0:T(1024)S(1)}, f32[3584]{0:T(1024)}, u32[]{:S(2)}) copy-start(f32[3584]{0:T(1024)} %param.39) | copy-start | bytes 43012
  455.1 1.0 copy-start.4
  455.1 1.2 copy-start.5
  456.1 5.0 copy-start.25
  459.2 63.7 %copy-start.20 = (f32[448]{0:T(512)S(1)}, f32[448]{0:T(512)}, u32[]{:S(2)}) copy-start(f32[448]{0:T(512)} %param.43) | copy-start | bytes 5380
  461.0 65.9 %copy-start.1 = (bf16[448,3584]{1,0:T(8,128)(2,1)S(1)}, bf16[448,3584]{1,0:T(8,128)(2,1)}, u32[]{:S(2)}) copy-start(bf16[448,3584]{1,0:T(8,128)(2,1)} %param.37) | copy-start | bytes 9633796
Sparse Core Ops, SparseCore 0:
  29.2 88.2 all-gather.9
  227.9 90.6 all-reduce.1
  320.7 61.7 all-gather.5
  384.5 61.5 all-gather.7
  455.2 46.9 reduce-scatter.3
